TPU v7x, 32 devices: a whole 2x2x4 slice. The times are simulated.
32 devices in a mesh: group: 2 (over x), src: 16 (over z, y, core).
Axes of the slice: x: 2, y: 2, z: 4, core: 2. Of those that a mesh axis runs over, the one named last changes fastest.
Arguments:
- rcv_points: float32 [3, 4096], P(None, ('group', 'src')), parts along dimension 1, may hold values from -1 to 1
- rcv_normals: float32 [3, 4096], P(None, ('group', 'src')), parts along dimension 1, may hold values from -4 to 4
- left_modes: float32 [8, 4096], P(None, ('group', 'src')), parts along dimension 1, may hold values from -5 to 5
- vertices: float32 [3, 2048], P(None, ('group', 'src')), parts along dimension 1, may hold values from -1 to 1
- connect: int32 [2, 4096], P(None, ('group', 'src')), parts along dimension 1, may hold values from 0 to 1023, as said below
- right_modes: float32 [8, 4096], P(None, ('group', 'src')), parts along dimension 1, may hold values from -0.125 to 0.125
- mode_weights: float32 [16], P('group'), parts along dimension 0, may hold values from 0.25 to 1
Outputs:
- rcv_grad: float32 [6, 4096], P(None, ('group', 'src')), parts along dimension 1
- vert_grad: float32 [3, 2048], P(None, ('group', 'src')), parts along dimension 1
There are 2 independent parts, one for each index of `group`. A program takes and returns all parts, laid end to end along the dimension named above; each array names one. Nothing has to cross between parts.
Inputs may be any that keep to these rules, and one draw needn't show every extreme that they name: `connect`: a panel's first vertex is one of the 64 vertices held at the same index of src as the panel, and its second vertex is the next vertex number.
All inputs are finite; a program needn't handle non-finite values.
Results may differ from a plain program's by a relative error of at most 0.0003.
Values sent between devices are 32-bit elements; how exact they have to be, the bound alone decides.
No kernel may reach another device: no remote copies, remote signals or barrier semaphores. Data moves between devices by JAX's collectives and lax.ppermute only.
A program may use at most 64 MiB of HBM per device.

v0:
```python
import math
import jax
import jax.numpy as jnp
from jax import lax
from jax.sharding import PartitionSpec as P

core_term = 0.05
inverse_four_pi = 0.25 / math.pi


def shifted(value, axis, steps):
    count = lax.axis_size(axis)
    leading, last = (max(0, -steps), min(count, count - steps))
    return lax.ppermute(value, axis, [(source, source + steps) for source in range(leading, last)])


def lift_points(raw):
    return jnp.stack([raw[0], raw[1], 0.5 + 0.2 * raw[2]])


def place_points(raw):
    return jnp.stack([raw[0], raw[1], 0.2 * raw[2]])


def tile_energy(points, normals, first_end, second_end, coefficient):
    rel_first = points[:, None, :] - first_end[:, :, None]
    rel_second = points[:, None, :] - second_end[:, :, None]
    segment = (second_end - first_end)[:, :, None]
    cross_x = rel_first[1] * rel_second[2] - rel_first[2] * rel_second[1]
    cross_y = rel_first[2] * rel_second[0] - rel_first[0] * rel_second[2]
    cross_z = rel_first[0] * rel_second[1] - rel_first[1] * rel_second[0]
    cross_sq = cross_x * cross_x + cross_y * cross_y + cross_z * cross_z
    dist_first = jnp.sqrt(jnp.sum(rel_first * rel_first, axis=0))
    dist_second = jnp.sqrt(jnp.sum(rel_second * rel_second, axis=0))
    along_term = jnp.sum(segment * (rel_first / dist_first - rel_second / dist_second), axis=0)
    span_sq = jnp.sum(segment * segment, axis=0)
    denominator = cross_sq + core_term * (span_sq + 1.0)
    normal_term = (
        normals[0][None, :] * cross_x
        + normals[1][None, :] * cross_y
        + normals[2][None, :] * cross_z
    )
    influence = inverse_four_pi * normal_term * along_term / denominator
    return jnp.sum(coefficient * influence)


def tile_gradients(points, normals, first_end, second_end, coefficient):
    return jax.grad(tile_energy, argnums=(0, 1, 2, 3))(
        points, normals, first_end, second_end, coefficient
    )


def on_device(rcv_points, rcv_normals, left_modes, vertices, connect, right_modes, mode_weights):
    own_count = vertices.shape[1]
    next_first = shifted(vertices[:, :1], "src", -1)
    extended = jnp.concatenate([vertices, next_first], axis=1)
    places = place_points(extended)
    base_vertex = lax.axis_index("src") * own_count
    local_first = connect[0] - base_vertex
    local_second = local_first + 1
    first_end = places[:, local_first]
    second_end = places[:, local_second]
    points = lift_points(rcv_points)
    chain_scale = jnp.array([1.0, 1.0, 0.2], dtype=jnp.float32)[:, None]
    weighted = right_modes * mode_weights[:, None]
    receiver_count = rcv_points.shape[1] * lax.axis_size("src")
    source_count = connect.shape[1]
    start_totals = (
        jnp.zeros((3, source_count), jnp.float32),
        jnp.zeros((3, source_count), jnp.float32),
        jnp.zeros((6, receiver_count), jnp.float32),
    )
    shard_points = lax.all_gather(points, "src", axis=1, tiled=True)
    shard_normals = lax.all_gather(rcv_normals, "src", axis=1, tiled=True)
    shard_left = lax.all_gather(left_modes, "src", axis=1, tiled=True)
    row_count = shard_points.shape[1]
    width_rows = math.gcd(row_count, 2048)

    def advance(number, inner):
        sum_first, sum_second, receiver_buffer = inner
        local_start = number * width_rows
        block_points = lax.dynamic_slice_in_dim(shard_points, local_start, width_rows, 1)
        block_normals = lax.dynamic_slice_in_dim(shard_normals, local_start, width_rows, 1)
        block_left = lax.dynamic_slice_in_dim(shard_left, local_start, width_rows, 1)
        coefficient = jnp.einsum("mj,mi->ji", weighted, block_left, precision=lax.Precision.HIGHEST)
        grads = tile_gradients(block_points, block_normals, first_end, second_end, coefficient)
        rows_out = jnp.concatenate([grads[0] * chain_scale, grads[1]], axis=0)
        receiver_buffer = lax.dynamic_update_slice_in_dim(receiver_buffer, rows_out, local_start, 1)
        return (sum_first + grads[2], sum_second + grads[3], receiver_buffer)

    sum_first, sum_second, receiver_buffer = lax.fori_loop(
        0, row_count // width_rows, advance, start_totals
    )
    rcv_grad = lax.psum_scatter(receiver_buffer, "src", scatter_dimension=1, tiled=True)
    vertex_partial = jnp.zeros((3, own_count + 1), jnp.float32)
    vertex_partial = (
        vertex_partial.at[:, local_first].add(sum_first).at[:, local_second].add(sum_second)
    )
    incoming = shifted(vertex_partial[:, own_count:], "src", 1)
    own_part = vertex_partial[:, :own_count]
    own_part = jnp.concatenate([own_part[:, :1] + incoming, own_part[:, 1:]], axis=1)
    vert_grad = own_part * chain_scale
    return (rcv_grad, vert_grad)


def solution(mesh):
    in_specs = (
        P(None, ("group", "src")),
        P(None, ("group", "src")),
        P(None, ("group", "src")),
        P(None, ("group", "src")),
        P(None, ("group", "src")),
        P(None, ("group", "src")),
        P("group"),
    )
    out_specs = (P(None, ("group", "src")), P(None, ("group", "src")))
    return jax.shard_map(
        on_device, mesh=mesh, in_specs=in_specs, out_specs=out_specs, check_vma=False
    )
```

profile of v0, /device:TPU:0, one launch (start us, length us, event | category | flops | bytes accessed | tf_op | source)
XLA Modules:
  0.0 154.4 jit_solution(849035136935577808)
XLA Ops:
  7.2 1.3 collective-permute-start
  8.5 0.7 multiply_add_fusion.1
  9.2 0.7 slice.81
  9.9 23.8 %all_gather.10 = f32[3,2048]{1,0:T(4,128)S(1)} all-gather(f32[3,128]{1,0:T(4,128)S(1)} %pad_maximum_fusion.3), channel_id=1, replica_groups=mesh['group'=2,'src'=16] {'src'}, dimensions={1}, use_global_device_ids=true | all-gather | bytes 26112 | tf_op jit(solution)/shard_map/all_gather | solution.py:73
  33.7 17.7 %all_gather.9 = f32[3,2048]{1,0:T(4,128)S(1)} all-gather(f32[3,128]{1,0:T(4,128)} %param.9), channel_id=1, replica_groups=mesh['group'=2,'src'=16] {'src'}, dimensions={1}, use_global_device_ids=true | all-gather | bytes 26112 | tf_op jit(solution)/shard_map/all_gather | solution.py:74
  51.4 19.2 %all_gather.11 = f32[8,2048]{1,0:T(8,128)S(1)} all-gather(f32[8,128]{1,0:T(8,128)} %param.10), channel_id=1, replica_groups=mesh['group'=2,'src'=16] {'src'}, dimensions={1}, use_global_device_ids=true | all-gather | bytes 69632 | tf_op jit(solution)/shard_map/all_gather | solution.py:75
  70.6 0.7 fusion.24
  71.3 0.8 pad_maximum_fusion.1
  72.1 0.1 copy.26
  72.2 0.6 gather_fusion.1
  72.9 0.7 gather_fusion
  73.7 0.8 fusion.15
  74.6 0.3 multiply_divide_fusion.1
  74.9 0.3 multiply_divide_fusion.2
  75.3 1.8 %divide_multiply_fusion.1 = (f32[128,2048]{1,0:T(8,128)S(1)}, f32[128,2048]{1,0:T(8,128)S(1)}, f32[128,2048]{1,0:T(8,128)S(1)}, f32[128,2048]{1,0:T(8,128)S(1)},...) fusion(f32[128]{0:T(128)S(1)} %add_multiply_fusion.2, f32[2048]{0:T(1024)S(1)} %bitcast.136, ...), kind=kOutput, calls=%fused_computation.109 | convolution fusion | flops 31196160 | bytes 13726240 | tf_op jit(solution)/shard_map/while/body/eval_jaxpr/mj,mi->ji/dot_general | solution.py:85
  77.1 2.5 %multiply_reduce_fusion = (f32[3,128]{1,0:T(4,128)S(1)}, f32[128,2048]{1,0:T(8,128)S(1)}, f32[128,2048]{1,0:T(8,128)S(1)}, f32[128,2048]{1,0:T(8,128)S(1)}) fusion(f32[128,2048]{1,0:T(8,128)S(1)} %get-tuple-element.62, f32[128,2048]{1,0:T(8,128)S(1)} %get-tuple-element.92, f32[3,128]{1,0:T(4,128)S(1)} %bitcast.127, f32[128,2048]{1,0:T(8,128)S(1)} %get-tuple-element.94, ...), kind=kLoop, calls=%fused_computation.36 | loop fusion | flops 12582528 | bytes 8419328 | tf_op jit(solution)/shard_map/while/body/eval_jaxpr/transpose(jvp())/reduce_sum | solution.py:35
  79.6 0.2 multiply_multiply_fusion.3
  79.8 0.2 multiply_multiply_fusion.1
  80.1 0.6 fusion.28
  80.6 2.0 %multiply_bitcast_fusion.5 = (f32[1,128,2048]{2,1,0:T(8,128)}, f32[128,2048]{1,0:T(8,128)}, f32[128,2048]{1,0:T(8,128)S(1)}) fusion(f32[3,128,2048]{2,1,0:T(8,128)S(1)} %get-tuple-element.95, f32[128,2048]{1,0:T(8,128)S(1)} %get-tuple-element.67, f32[128,2048]{1,0:T(8,128)S(1)} %get-tuple-element.54, f32[2048]{0:T(1024)S(1)} %broadcast_multiply_fusion.2, ...), kind=kLoop, calls=%fused_computation.57 | loop fusion | flops 2359296 | bytes 9445376 | tf_op jit(solution)/shard_map/while/body/eval_jaxpr/transpose(jvp())/broadcast_in_dim | solution.py:31
  82.6 2.2 %multiply_bitcast_fusion.3 = (f32[1,128,2048]{2,1,0:T(8,128)S(1)}, f32[128,2048]{1,0:T(8,128)}, f32[1,128,2048]{2,1,0:T(8,128)S(1)}, f32[128,2048]{1,0:T(8,128)}...) fusion(f32[3,128,2048]{2,1,0:T(8,128)S(1)} %get-tuple-element.95, f32[128,2048]{1,0:T(8,128)S(1)} %get-tuple-element.66, ...), kind=kLoop, calls=%fused_computation.55 | loop fusion | flops 5236736 | bytes 11575296 | tf_op jit(solution)/shard_map/while/body/eval_jaxpr/transpose(jvp())/broadcast_in_dim | solution.py:30
  84.9 4.8 %multiply_bitcast_fusion.11 = (f32[1,128,2048]{2,1,0:T(8,128)S(1)}, f32[1,128,2048]{2,1,0:T(8,128)S(1)}, f32[1,128,2048]{2,1,0:T(8,128)S(1)}, f32[1,128,2048]{2,...) fusion(f32[128,2048]{1,0:T(8,128)} %get-tuple-element.56, ...), kind=kLoop, calls=%fused_computation.65 | loop fusion | flops 3145728 | bytes 18874368 | tf_op jit(solution)/shard_map/while/body/eval_jaxpr/transpose(jvp())/broadcast_in_dim | solution.py:31
  89.7 3.4 %fusion.27 = (f32[3,128]{1,0:T(4,128)S(1)}, f32[3,2048]{1,0:T(4,128)S(1)}) fusion(f32[1,128,2048]{2,1,0:T(8,128)} %get-tuple-element.88, f32[1,128,2048]{2,1,0:T(8,128)S(1)} %get-tuple-element.70, f32[1,128,2048]{2,1,0:T(8,128)} %get-tuple-element.89, f32[1,128,2048]{2,1,0:T(8,128)S(1)} %get-tuple-element.58, f32[1,128,2048]{2,1,0:T(8,128)} %get-tuple-element.90, ...), kind=kLoop, calls=%fused_computation.111 | loop fusion | flops 11003520 | bytes 9490944 | tf_op jit(solution)/shard_map/while/body/eval_jaxpr/transpose(jvp())/reduce_sum | solution.py:26
  93.1 1.9 %fusion.26 = (f32[3,128]{1,0:T(4,128)S(1)}, f32[3,2048]{1,0:T(4,128)S(1)}) fusion(f32[1,128,2048]{2,1,0:T(8,128)S(1)} %get-tuple-element.84, f32[1,128,2048]{2,1,0:T(8,128)S(1)} %get-tuple-element.85, f32[1,128,2048]{2,1,0:T(8,128)S(1)} %get-tuple-element.86, f32[1,128,2048]{2,1,0:T(8,128)S(1)} %copy-done, f32[1,128,2048]{2,1,0:T(8,128)S(1)} %get-tuple-element.73, ...), kind=kLoop, calls=%fused_computation.110 | loop fusion | flops 11789952 | bytes 9490944 | tf_op jit(solution)/shard_map/while/body/eval_jaxpr/transpose(jvp())/reduce_sum | solution.py:27
  95.0 0.1 copy.31
  95.2 1.0 scatter_custom_fusion
  96.2 1.2 scatter_fusion
  97.6 0.6 pad_maximum_fusion
  98.3 2.2 %collective-permute-start.1 = (f32[3,1]{0,1:T(1,128)S(1)}, f32[3,1]{0,1:T(1,128)S(1)}, u32[]{:S(2)}, u32[]{:S(2)}) collective-permute-start(f32[3,1]{0,1:T(1,128)S(1)} %slice.108), channel_id=1, source_target_pairs={{0,1},{1,2},{2,3},{3,4},{4,5},{5,6},{6,7},{7,8},{8,9},{9,10},{10,1... | collective-permute-start | bytes 44 | tf_op jit(solution)/shard_map/ppermute | solution.py:14
  100.6 0.7 collective-permute-done.1
  101.4 0.7 maximum_multiply_fusion
  102.1 45.5 %reduce-scatter.2.cloned.1.call-done = f32[6,128]{1,0:T(8,128)} async-done(((f32[6,2048]{1,0:T(8,128)}), f32[6,128]{1,0:T(8,128)}) %reduce-scatter.2.cloned.1.call-update) | async-done | bytes 3088 | tf_op jit(solution)/shard_map/reduce_scatter | solution.py:94
  (33 shorter events, 0.7 us)
Async XLA Ops:
  7.2 140.4 %reduce-scatter.2.cloned.1.call-start = ((), (), s32[]{:S(2)}) async-start(), calls=%async_computation.1 | async-start | bytes 69632 | tf_op jit(solution)/shard_map/reduce_scatter | solution.py:94
  7.2 64.1 %collective-permute-start = (f32[3,1]{1,0:T(4,128)}, f32[3,1]{1,0:T(4,128)S(1)}, u32[]{:S(2)}, u32[]{:S(2)}) collective-permute-start(f32[3,1]{1,0:T(4,128)} %bitcast.141), channel_id=1, source_target_pairs={{1,0},{2,1},{3,2},{4,3},{5,4},{6,5},{7,6},{8,7},{9,8},{10,9},{11,1... | collective-permute-start | bytes 44 | tf_op jit(solution)/shard_map/ppermute | solution.py:14
  74.5 0.7 copy-start.2
  74.5 0.7 copy-start.3
  89.7 3.4 %copy-start = (f32[1,128,2048]{2,1,0:T(8,128)S(1)}, f32[1,128,2048]{2,1,0:T(8,128)}, u32[]{:S(2)}) copy-start(f32[1,128,2048]{2,1,0:T(8,128)} %get-tuple-element.87) | copy-start | bytes 3145732
  93.1 4.4 %copy-start.1 = (f32[3]{0:T(128)S(1)}, f32[3]{0:T(128)}, u32[]{:S(2)}) copy-start(f32[3]{0:T(128)} %constant.34.clone) | copy-start | bytes 40
  98.3 3.1 %collective-permute-start.1 = (f32[3,1]{0,1:T(1,128)S(1)}, f32[3,1]{0,1:T(1,128)S(1)}, u32[]{:S(2)}, u32[]{:S(2)}) collective-permute-start(f32[3,1]{0,1:T(1,128)S(1)} %slice.108), channel_id=1, source_target_pairs={{0,1},{1,2},{2,3},{3,4},{4,5},{5,6},{6,7},{7,8},{8,9},{9,10},{10,1... | collective-permute-start | bytes 44 | tf_op jit(solution)/shard_map/ppermute | solution.py:14
Sparse Core Ops, SparseCore 0:
  98.4 49.1 reduce-scatter.1
where the time goes:
time: 155 us; the launch traced here: 154 us
  blocking collectives  60.7 us (39%)
  waiting for transfers between devices  46.3 us (30%)
  other arithmetic  25.1 us (16%)
  between operations  14.3 us (9%)
  starting transfers between devices  3.57 us (2%)
  local copies, waits for them, and re-layouts  2.68 us (2%)
  matrix products  1.85 us (1%)
    reduce_scatter x1, waiting for transfers between devices, on_device(): lax.psum_scatter(receiver_buffer, 'src', scatter_dimension=1, tiled=True)  45.5 us
    all_gather x1, blocking collectives, on_device(): shard_points = lax.all_gather(points, 'src', axis=1, tiled=True)  23.8 us
    all_gather x1, blocking collectives, on_device(): shard_left = lax.all_gather(left_modes, 'src', axis=1, tiled=True)  19.2 us
    all_gather x1, blocking collectives, on_device(): shard_normals = lax.all_gather(rcv_normals, 'src', axis=1, tiled=True)  17.7 us
    broadcast_in_dim x2, other arithmetic, tile_energy(): cross_z = rel_first[0] * rel_second[1] - rel_first[1] * rel_second[0]  6.79 us
    ppermute x2, starting transfers between devices, shifted(): lax.ppermute(value, axis, [(source, source + steps) for source in range(l...  3.54 us
    reduce_sum x1, other arithmetic, tile_energy(): rel_first = points[:, None, :] - first_end[:, :, None]  3.41 us
  transfers between devices with their start and end apart: 3, of which 2 were waited for; matrix products, arithmetic and copies ran while one was open for 2% of the time, Pallas kernels for 0%

commit v1 on v0

--- a/solution.py
+++ b/solution.py
@@ -70,8 +70,11 @@
         jnp.zeros((3, source_count), jnp.float32),
         jnp.zeros((6, receiver_count), jnp.float32),
     )
-    shard_points = lax.all_gather(points, "src", axis=1, tiled=True)
-    shard_normals = lax.all_gather(rcv_normals, "src", axis=1, tiled=True)
+    shard_points, shard_normals = jnp.split(
+        lax.all_gather(jnp.concatenate([points, rcv_normals], axis=0), "src", axis=1, tiled=True),
+        [points.shape[0]],
+        axis=0,
+    )
     shard_left = lax.all_gather(left_modes, "src", axis=1, tiled=True)
     row_count = shard_points.shape[1]
     width_rows = math.gcd(row_count, 2048)

time: 155 us -> 138 us (0.89)
  blocking collectives: 60.7 us -> 41.8 us
    all_gather x2 -> x1, blocking collectives: 41.5 us -> 23.9 us  [on_device(): lax.all_gather(jnp.concatenate([points, rcv_normals], axis=0), 'src', axi...]
  transfers between devices with their start and end apart: 3 -> 3, of which waited for: 2 -> 2; matrix products, arithmetic and copies ran while one was open for 2% -> 3% of each run, Pallas kernels for 0% -> 0%
where the time goes in v1:
time: 138 us; the launch traced here: 137 us
  waiting for transfers between devices  47.3 us (34%)
  blocking collectives  41.8 us (30%)
  other arithmetic  25.8 us (19%)
  between operations  14.3 us (10%)
  starting transfers between devices  3.57 us (3%)
  local copies, waits for them, and re-layouts  2.69 us (2%)
  matrix products  1.86 us (1%)
    reduce_scatter x1, waiting for transfers between devices, on_device(): lax.psum_scatter(receiver_buffer, 'src', scatter_dimension=1, tiled=True)  46.5 us
    all_gather x1, blocking collectives, on_device(): lax.all_gather(jnp.concatenate([points, rcv_normals], axis=0), 'src', axi...  23.9 us
    all_gather x1, blocking collectives, on_device(): shard_left = lax.all_gather(left_modes, 'src', axis=1, tiled=True)  17.9 us
    broadcast_in_dim x2, other arithmetic, tile_energy(): cross_z = rel_first[0] * rel_second[1] - rel_first[1] * rel_second[0]  6.79 us
    ppermute x2, starting transfers between devices, shifted(): lax.ppermute(value, axis, [(source, source + steps) for source in range(l...  3.54 us
    reduce_sum x1, other arithmetic, tile_energy(): rel_first = points[:, None, :] - first_end[:, :, None]  3.41 us
  transfers between devices with their start and end apart: 3, of which 2 were waited for; matrix products, arithmetic and copies ran while one was open for 3% of the time, Pallas kernels for 0%

profile of v1, /device:TPU:0, one launch (start us, length us, event | category | flops | bytes accessed | tf_op | source)
XLA Modules:
  0.0 137.2 jit_solution(15015483532067476208)
XLA Ops:
  7.2 1.3 collective-permute-start
  8.5 0.7 multiply_add_fusion.1
  9.2 0.7 slice.83
  9.9 0.7 pad_maximum_fusion.1
  10.6 23.9 %all_gather.6 = f32[6,2048]{1,0:T(8,128)S(1)} all-gather(f32[6,128]{1,0:T(8,128)S(1)} %pad_maximum_fusion.1), channel_id=1, replica_groups=mesh['group'=2,'src'=16] {'src'}, dimensions={1}, use_global_device_ids=true | all-gather | bytes 52224 | tf_op jit(solution)/shard_map/all_gather | solution.py:74
  34.5 17.9 %all_gather.7 = f32[8,2048]{1,0:T(8,128)S(1)} all-gather(f32[8,128]{1,0:T(8,128)} %param.10), channel_id=1, replica_groups=mesh['group'=2,'src'=16] {'src'}, dimensions={1}, use_global_device_ids=true | all-gather | bytes 69632 | tf_op jit(solution)/shard_map/all_gather | solution.py:78
  52.4 0.7 fusion.24
  53.1 0.8 pad_maximum_fusion.2
  53.9 0.1 copy.26
  54.0 0.6 gather_fusion.1
  54.7 0.7 gather_fusion
  55.5 0.8 fusion.15
  56.3 0.3 multiply_divide_fusion.1
  56.7 0.3 multiply_divide_fusion.2
  57.1 1.9 %divide_multiply_fusion.1 = (f32[128,2048]{1,0:T(8,128)S(1)}, f32[128,2048]{1,0:T(8,128)S(1)}, f32[128,2048]{1,0:T(8,128)S(1)}, f32[128,2048]{1,0:T(8,128)S(1)},...) fusion(f32[128]{0:T(128)S(1)} %add_multiply_fusion.2, f32[2048]{0:T(1024)S(1)} %bitcast.136, ...), kind=kOutput, calls=%fused_computation.109 | convolution fusion | flops 31196160 | bytes 13726240 | tf_op jit(solution)/shard_map/while/body/eval_jaxpr/mj,mi->ji/dot_general | solution.py:88
  58.9 2.5 %multiply_reduce_fusion = (f32[3,128]{1,0:T(4,128)S(1)}, f32[128,2048]{1,0:T(8,128)S(1)}, f32[128,2048]{1,0:T(8,128)S(1)}, f32[128,2048]{1,0:T(8,128)S(1)}) fusion(f32[128,2048]{1,0:T(8,128)S(1)} %get-tuple-element.62, f32[128,2048]{1,0:T(8,128)S(1)} %get-tuple-element.92, f32[3,128]{1,0:T(4,128)S(1)} %bitcast.127, f32[128,2048]{1,0:T(8,128)S(1)} %get-tuple-element.94, ...), kind=kLoop, calls=%fused_computation.36 | loop fusion | flops 12582528 | bytes 8419328 | tf_op jit(solution)/shard_map/while/body/eval_jaxpr/transpose(jvp())/reduce_sum | solution.py:35
  61.4 0.2 multiply_multiply_fusion.3
  61.6 0.2 multiply_multiply_fusion.1
  61.8 0.6 fusion.28
  62.4 2.0 %multiply_bitcast_fusion.5 = (f32[1,128,2048]{2,1,0:T(8,128)}, f32[128,2048]{1,0:T(8,128)}, f32[128,2048]{1,0:T(8,128)S(1)}) fusion(f32[3,128,2048]{2,1,0:T(8,128)S(1)} %get-tuple-element.98, f32[128,2048]{1,0:T(8,128)S(1)} %get-tuple-element.67, f32[128,2048]{1,0:T(8,128)S(1)} %get-tuple-element.54, f32[2048]{0:T(1024)S(1)} %broadcast_multiply_fusion.2, ...), kind=kLoop, calls=%fused_computation.57 | loop fusion | flops 2359296 | bytes 9445376 | tf_op jit(solution)/shard_map/while/body/eval_jaxpr/transpose(jvp())/broadcast_in_dim | solution.py:31
  64.4 2.2 %multiply_bitcast_fusion.3 = (f32[1,128,2048]{2,1,0:T(8,128)S(1)}, f32[128,2048]{1,0:T(8,128)}, f32[1,128,2048]{2,1,0:T(8,128)S(1)}, f32[128,2048]{1,0:T(8,128)}...) fusion(f32[3,128,2048]{2,1,0:T(8,128)S(1)} %get-tuple-element.98, f32[128,2048]{1,0:T(8,128)S(1)} %get-tuple-element.66, ...), kind=kLoop, calls=%fused_computation.55 | loop fusion | flops 5236736 | bytes 11575296 | tf_op jit(solution)/shard_map/while/body/eval_jaxpr/transpose(jvp())/broadcast_in_dim | solution.py:30
  66.7 4.8 %multiply_bitcast_fusion.11 = (f32[1,128,2048]{2,1,0:T(8,128)S(1)}, f32[1,128,2048]{2,1,0:T(8,128)S(1)}, f32[1,128,2048]{2,1,0:T(8,128)S(1)}, f32[1,128,2048]{2,...) fusion(f32[128,2048]{1,0:T(8,128)} %get-tuple-element.56, ...), kind=kLoop, calls=%fused_computation.65 | loop fusion | flops 3145728 | bytes 18874368 | tf_op jit(solution)/shard_map/while/body/eval_jaxpr/transpose(jvp())/broadcast_in_dim | solution.py:31
  71.5 3.4 %fusion.27 = (f32[3,128]{1,0:T(4,128)S(1)}, f32[3,2048]{1,0:T(4,128)S(1)}) fusion(f32[1,128,2048]{2,1,0:T(8,128)} %get-tuple-element.88, f32[1,128,2048]{2,1,0:T(8,128)S(1)} %get-tuple-element.70, f32[1,128,2048]{2,1,0:T(8,128)} %get-tuple-element.89, f32[1,128,2048]{2,1,0:T(8,128)S(1)} %get-tuple-element.58, f32[1,128,2048]{2,1,0:T(8,128)} %get-tuple-element.90, ...), kind=kLoop, calls=%fused_computation.111 | loop fusion | flops 11003520 | bytes 9490944 | tf_op jit(solution)/shard_map/while/body/eval_jaxpr/transpose(jvp())/reduce_sum | solution.py:26
  74.9 1.9 %fusion.26 = (f32[3,128]{1,0:T(4,128)S(1)}, f32[3,2048]{1,0:T(4,128)S(1)}) fusion(f32[1,128,2048]{2,1,0:T(8,128)S(1)} %get-tuple-element.84, f32[1,128,2048]{2,1,0:T(8,128)S(1)} %get-tuple-element.85, f32[1,128,2048]{2,1,0:T(8,128)S(1)} %get-tuple-element.86, f32[1,128,2048]{2,1,0:T(8,128)S(1)} %copy-done, f32[1,128,2048]{2,1,0:T(8,128)S(1)} %get-tuple-element.73, ...), kind=kLoop, calls=%fused_computation.110 | loop fusion | flops 11789952 | bytes 9490944 | tf_op jit(solution)/shard_map/while/body/eval_jaxpr/transpose(jvp())/reduce_sum | solution.py:27
  76.8 0.1 copy.31
  77.0 1.0 scatter_custom_fusion
  78.0 1.2 scatter_fusion
  79.4 0.6 pad_maximum_fusion
  80.1 2.2 %collective-permute-start.1 = (f32[3,1]{0,1:T(1,128)S(1)}, f32[3,1]{0,1:T(1,128)S(1)}, u32[]{:S(2)}, u32[]{:S(2)}) collective-permute-start(f32[3,1]{0,1:T(1,128)S(1)} %slice.111), channel_id=1, source_target_pairs={{0,1},{1,2},{2,3},{3,4},{4,5},{5,6},{6,7},{7,8},{8,9},{9,10},{10,1... | collective-permute-start | bytes 44 | tf_op jit(solution)/shard_map/ppermute | solution.py:14
  82.4 0.7 collective-permute-done.1
  83.2 0.7 maximum_multiply_fusion
  83.9 46.5 %reduce-scatter.2.cloned.1.call-done = f32[6,128]{1,0:T(8,128)} async-done(((f32[6,2048]{1,0:T(8,128)}), f32[6,128]{1,0:T(8,128)}) %reduce-scatter.2.cloned.1.call-update) | async-done | bytes 3088 | tf_op jit(solution)/shard_map/reduce_scatter | solution.py:97
  (33 shorter events, 0.7 us)
Async XLA Ops:
  7.2 123.2 %reduce-scatter.2.cloned.1.call-start = ((), (), s32[]{:S(2)}) async-start(), calls=%async_computation.1 | async-start | bytes 69632 | tf_op jit(solution)/shard_map/reduce_scatter | solution.py:97
  7.2 45.9 %collective-permute-start = (f32[3,1]{1,0:T(4,128)}, f32[3,1]{1,0:T(4,128)S(1)}, u32[]{:S(2)}, u32[]{:S(2)}) collective-permute-start(f32[3,1]{1,0:T(4,128)} %bitcast.141), channel_id=1, source_target_pairs={{1,0},{2,1},{3,2},{4,3},{5,4},{6,5},{7,6},{8,7},{9,8},{10,9},{11,1... | collective-permute-start | bytes 44 | tf_op jit(solution)/shard_map/ppermute | solution.py:14
  56.3 0.7 copy-start.2
  56.3 0.7 copy-start.3
  71.5 3.4 %copy-start = (f32[1,128,2048]{2,1,0:T(8,128)S(1)}, f32[1,128,2048]{2,1,0:T(8,128)}, u32[]{:S(2)}) copy-start(f32[1,128,2048]{2,1,0:T(8,128)} %get-tuple-element.87) | copy-start | bytes 3145732
  74.9 4.4 %copy-start.1 = (f32[3]{0:T(128)S(1)}, f32[3]{0:T(128)}, u32[]{:S(2)}) copy-start(f32[3]{0:T(128)} %constant.34.clone) | copy-start | bytes 40
  80.1 3.1 %collective-permute-start.1 = (f32[3,1]{0,1:T(1,128)S(1)}, f32[3,1]{0,1:T(1,128)S(1)}, u32[]{:S(2)}, u32[]{:S(2)}) collective-permute-start(f32[3,1]{0,1:T(1,128)S(1)} %slice.111), channel_id=1, source_target_pairs={{0,1},{1,2},{2,3},{3,4},{4,5},{5,6},{6,7},{7,8},{8,9},{9,10},{10,1... | collective-permute-start | bytes 44 | tf_op jit(solution)/shard_map/ppermute | solution.py:14
Sparse Core Ops, SparseCore 0:
  80.2 50.1 reduce-scatter.1
